TPU v7x, 128 devices: a whole 4x4x4 slice. The times are simulated.
128 devices in a mesh: row: 8 (over y, x_hi), col: 16 (over x_lo, z, core).
Axes of the slice: x: 4 (x_hi: 2, x_lo: 2; x = x_hi * 2 + x_lo), y: 4, z: 4, core: 2. Of those that a mesh axis runs over, the one named last changes fastest.
Arguments:
- local_ops: bfloat16 [8, 16, 2048, 2048], P('row', 'col'), may hold values from -2 to 30, as said below
- loads: float32 [8, 16, 2048, 256], P('row', 'col'), may hold values from -6 to 6
- modes: float32 [8, 16, 32, 2048], P('row', 'col'), may hold values from -1 to 1
- coarse_inverse: float32 [4096, 4096], P('row', 'col'), may hold values from -1 to 1
- face_rows: int32 [8, 16, 4, 512], P('row', 'col'), may hold values from 0 to 2047, as said below
- adjacency: int32 [8, 16, 4], P('row', 'col'), may hold values from 0 to 1, as said below
- contact: int32 [8, 16, 2048], P('row', 'col'), may hold values 0 or 1
Outputs:
- multipliers: float32 [8, 16, 2048, 256], P('row', 'col')
Inputs may be any that keep to these rules, and one draw needn't show every extreme that they name: `face_rows`: for each subdomain the 2048 entries are a permutation of 0 to 2047. `adjacency`: symmetric across each shared face (a subdomain's south flag equals the north flag of the one below it, its east flag the west flag of the one to its right); 0 on faces at the grid's edge. `local_ops`: each subdomain's local dual operator is symmetric positive definite.
All inputs are finite; a program needn't handle non-finite values. No bound on the sum of `contact` on one device may be relied on, other than what follows from the above.
Results may differ from a plain program's by a relative error of at most 0.00099.
Values sent between devices are 32-bit elements; how exact they have to be, the bound alone decides.
A program may use at most 128 MiB of HBM per device.

v0:
```python
import functools
import jax
import jax.numpy as jnp
from jax import lax
from jax.sharding import Mesh
from jax.sharding import PartitionSpec as P

ITERS = 2
ROW = ("row_0", "row_1")
COL = ("col_0", "col_1", "col_2")
ROW_COL = ("row_0", "row_1", "col_0", "col_1", "col_2")


def extended(block, sides, width):
    for axis, dim in sides:
        count = lax.axis_size(axis)
        forward = [(i, i + 1) for i in range(count - 1)]
        backward = [(target, source) for source, target in forward]
        low = lax.ppermute(
            lax.slice_in_dim(block, block.shape[dim] - width, None, axis=dim), axis, forward
        )
        high = lax.ppermute(lax.slice_in_dim(block, 0, width, axis=dim), axis, backward)
        block = jnp.concatenate([low, block, high], axis=dim)
    return block


def in_blocks(value, dim, devices):
    shape = value.shape
    blocks = value.reshape(*shape[:dim], devices, shape[dim] // devices, *shape[dim + 1 :])
    return jnp.moveaxis(blocks, dim, 0)


def summed_on_arrival(value, axis, dim):
    blocks = in_blocks(value, dim, lax.axis_size(axis))
    arrived = lax.all_to_all(blocks, axis, split_axis=0, concat_axis=0, tiled=True)
    return arrived.sum(axis=0)


def by_axis(value, axes):
    return functools.reduce(lax.psum, axes, value)


def per_device(local_ops, loads, modes, coarse_inverse, face_rows, adjacency, contact):
    local_op = local_ops[0, 0]
    load_term = loads[0, 0]
    mode_rows = modes[0, 0]
    row_index = face_rows[0, 0]
    adj_flags = adjacency[0, 0].astype(jnp.float32)
    face_size = row_index.shape[1]
    order = load_term.shape[0]
    case_count = load_term.shape[1]
    flat_rows = row_index.reshape(-1)
    free_face = jnp.repeat(1.0 - adj_flags, face_size)
    row_free = jnp.zeros((order,), jnp.float32).at[flat_rows].set(free_face)
    weight = 0.5 + 0.5 * row_free
    clamp_rows = contact[0, 0].astype(jnp.float32) * row_free > 0.5

    def assemble(field_values):
        blocks = jnp.take(field_values, row_index, axis=0)
        vertical = extended(blocks[0:2], ((ROW, 0),), 1)
        lateral = extended(blocks[2:4], ((COL, 0),), 1)
        incoming = (
            jnp.stack([vertical[0], vertical[3], lateral[0], lateral[3]]) * adj_flags[:, None, None]
        )
        return field_values.at[flat_rows].add(incoming.reshape(-1, case_count))

    multipliers = jnp.zeros((order, case_count), jnp.float32)
    for iteration in range(ITERS):
        if iteration == 0:
            local_term = -load_term
        else:
            local_term = (
                jnp.dot(
                    local_op, multipliers.astype(jnp.bfloat16), preferred_element_type=jnp.float32
                )
                - load_term
            )
        gradient = assemble(local_term)
        coarse_coef = jnp.dot(
            mode_rows, gradient, precision=lax.Precision.HIGHEST, preferred_element_type=jnp.float32
        )
        tile_cols = coarse_inverse.shape[1]
        col_index = lax.axis_index(COL)
        gathered = lax.all_gather(coarse_coef, ROW_COL, axis=0, tiled=True)
        coarse_block = lax.dynamic_slice_in_dim(gathered, col_index * tile_cols, tile_cols, 0)
        coarse_amount = summed_on_arrival(
            jnp.dot(
                coarse_inverse,
                coarse_block,
                precision=lax.Precision.HIGHEST,
                preferred_element_type=jnp.float32,
            ),
            COL,
            0,
        )
        correction = lax.dot_general(
            mode_rows,
            coarse_amount,
            (((0,), (0,)), ((), ())),
            precision=lax.Precision.HIGHEST,
            preferred_element_type=jnp.float32,
        )
        direction = gradient - assemble(correction)
        direction_half = direction.astype(jnp.bfloat16)
        operated = jnp.dot(local_op, direction_half, preferred_element_type=jnp.float32)
        totals = (
            by_axis(jnp.sum(weight[:, None] * direction * direction, axis=0), ROW_COL),
            by_axis(jnp.sum(direction * operated, axis=0), ROW_COL),
        )
        step_length = totals[0] / totals[1]
        multipliers = multipliers - step_length[None, :] * direction
        multipliers = jnp.where(clamp_rows[:, None], jnp.maximum(multipliers, 0.0), multipliers)
    return multipliers[None, None]


def solution(mesh):
    torus = Mesh(mesh.devices.reshape(4, 2, 2, 4, 2), ("row_0", "row_1", "col_0", "col_1", "col_2"))
    return jax.shard_map(
        per_device,
        mesh=torus,
        in_specs=(
            P(ROW, COL, None, None),
            P(ROW, COL, None, None),
            P(ROW, COL, None, None),
            P(ROW, COL),
            P(ROW, COL, None, None),
            P(ROW, COL, None),
            P(ROW, COL, None),
        ),
        out_specs=P(ROW, COL, None, None),
        check_vma=False,
    )
```

profile of v0, /device:TPU:1, one launch (start us, length us, event | category | flops | bytes accessed | tf_op | source)
XLA Modules:
  0.0 553.5 jit_solution(13121661826302791065)
XLA Ops:
  14.7 8.6 %gather_fusion = f32[2048,256]{1,0:T(8,128)} fusion(f32[2048,256]{1,0:T(8,128)S(1)} %copy.45, s32[2048]{0:T(1024)S(1)} %broadcast_clamp_fusion), kind=kCustom, calls=%fused_computation.clone | custom fusion | bytes 4202496 | tf_op jit(solution)/shard_map/jit(_take)/gather | solution.py:59
  25.4 5.5 collective-permute-start
  41.4 13.2 %collective-permute-done.1 = f32[1,512,256]{2,1,0:T(8,128)S(1)} collective-permute-done((f32[1,512,256]{2,1,0:T(8,128)S(1)}, f32[1,512,256]{2,1,0:T(8,128)S(1)}, u32[]{:S(2)}, u32[]{:S(2)}) %collective-permute-start.1) | collective-permute-done | bytes 524320 | tf_op jit(solution)/shard_map/ppermute | solution.py:22
  56.5 12.7 %scatter_fusion = f32[2048,256]{1,0:T(8,128)S(1)} fusion(f32[2048,256]{1,0:T(8,128)S(1)} %copy.45, s32[2048]{0:T(1024)S(1)} %bitcast.116, f32[2048,256]{1,0:T(8,128)} %bitcast_multiply_fusion.3), kind=kCustom, calls=%fused_computation.5 | custom fusion | flops 524288 | bytes 6299648 | tf_op jit(solution)/shard_map/scatter-add | solution.py:65
  71.1 73.4 %all-gather.3.cloned.1.call-done = f32[4096,256]{1,0:T(8,128)} async-done(((f32[32,256]{1,0:T(8,128)}), f32[4096,256]{1,0:T(8,128)}) %all-gather.3.cloned.1.call-update) | async-done | bytes 4194320 | tf_op jit(solution)/shard_map/all_gather | solution.py:84
  151.2 9.7 %all-to-all-done = f32[16,32,256]{2,1,0:T(8,128)S(1)} async-done(((f32[16,32,256]{2,1,0:T(8,128)}), f32[16,32,256]{2,1,0:T(8,128)S(1)}, u32[]{:S(2)}, u32[]{:S(2)}) %all-to-all-start) | async-done | bytes 524320 | tf_op jit(solution)/shard_map/all_to_all | solution.py:35
  167.0 10.1 %gather_fusion.1 = f32[2048,256]{1,0:T(8,128)} fusion(f32[2048,256]{1,0:T(8,128)} %copy.48, s32[2048]{0:T(1024)S(1)} %broadcast_clamp_fusion), kind=kCustom, calls=%fused_computation.1.clone | custom fusion | bytes 4202496 | tf_op jit(solution)/shard_map/jit(_take)/gather | solution.py:59
  191.7 8.5 %scatter_custom_fusion = f32[2048]{0:T(1024)S(1)} fusion(s32[2048]{0:T(1024)S(1)} %bitcast.117, f32[2048]{0:T(1024)S(1)} %bitcast.128, f32[]{:T(128)} %constant.19.clone.1), kind=kCustom, calls=%fused_computation.70 | custom fusion | bytes 8196 | tf_op jit(solution)/shard_map/scatter | solution.py:54
  202.1 5.0 collective-permute-done.5
  211.1 12.7 %scatter_fusion.1 = f32[2048,256]{1,0:T(8,128)S(1)} fusion(f32[2048,256]{1,0:T(8,128)S(1)} %copy-done.1, s32[2048]{0:T(1024)S(1)} %bitcast.118, f32[2048,256]{1,0:T(8,128)} %bitcast_multiply_fusion.2), kind=kCustom, calls=%fused_computation.6 | custom fusion | flops 524288 | bytes 6299648 | tf_op jit(solution)/shard_map/scatter-add | solution.py:65
  228.3 6.7 %fusion.31 = f32[256]{0:T(256)S(1)} fusion(f32[2048,256]{0,1:T(8,128)S(1)} %get-tuple-element.29, bf16[1,1,2048,2048]{3,2,1,0:T(8,128)(2,1)} %param.9), kind=kOutput, calls=%fused_computation.41 | convolution fusion | flops 2149056256 | bytes 10486784 | tf_op jit(solution)/shard_map/dot_general | solution.py:105
  235.0 7.0 %all-reduce.3 = (f32[256]{0:T(256)S(1)}, f32[256]{0:T(256)S(1)}) all-reduce(f32[256]{0:T(256)S(1)} %get-tuple-element.28, f32[256]{0:T(256)S(1)} %fusion.31), channel_id=1, replica_groups=mesh['row_0'=4,'row_1'=2,'col_0'=2,'col_1'=4,'col_2'=2] {'row_0'}, use_global_device_ids=true, to_apply=%region_5.7 | all-reduce | flops 512 | bytes 4096 | tf_op jit(solution)/shard_map/psum | solution.py:40
  242.0 5.3 all-reduce.9
  247.3 4.6 all-reduce.7
  251.9 14.5 %all-reduce.1 = (f32[256]{0:T(256)S(1)}, f32[256]{0:T(256)S(1)}) all-reduce(f32[256]{0:T(256)S(1)} %get-tuple-element.20, f32[256]{0:T(256)S(1)} %get-tuple-element.21), channel_id=1, replica_groups=mesh['row_0'=4,'row_1'=2,'col_0'=2,'col_1'=4,'col_2'=2] {'col_1'}, use_global_device_ids=true, to_apply=%region_8.10 | all-reduce | flops 512 | bytes 4096 | tf_op jit(solution)/shard_map/psum | solution.py:40
  266.4 7.1 %all-reduce.5 = (f32[256]{0:T(256)S(1)}, f32[256]{0:T(256)S(1)}) all-reduce(f32[256]{0:T(256)S(1)} %get-tuple-element.8, f32[256]{0:T(256)S(1)} %get-tuple-element.9), channel_id=1, replica_groups=mesh['row_0'=4,'row_1'=2,'col_0'=2,'col_1'=4,'col_2'=2] {'col_2'}, use_global_device_ids=true, to_apply=%region_9.11 | all-reduce | flops 512 | bytes 4096 | tf_op jit(solution)/shard_map/psum | solution.py:40
  273.5 7.7 %fusion.21 = f32[2048,256]{0,1:T(8,128)} fusion(bf16[1,1,2048,2048]{3,2,1,0:T(8,128)(2,1)} %param.9, f32[1,1,2048,256]{2,3,1,0:T(8,128)S(1)} %copy-done.4, f32[2048,256]{0,1:T(8,128)} %copy-done.5, f32[256]{0:T(256)S(1)} %div.6, pred[2048]{0:T(1024)(128)(4,1)S(1)} %multiply_compare_fusion), kind=kOutput, calls=%fused_computation.26 | convolution fusion | flops 2150629376 | bytes 14683136 | tf_op jit(solution)/shard_map/dot_general | solution.py:73
  283.1 8.6 %gather_fusion.2 = f32[2048,256]{1,0:T(8,128)} fusion(f32[2048,256]{1,0:T(8,128)S(1)} %copy.52, s32[2048]{0:T(1024)S(1)} %broadcast_clamp_fusion), kind=kCustom, calls=%fused_computation.2.clone | custom fusion | bytes 4202496 | tf_op jit(solution)/shard_map/jit(_take)/gather | solution.py:59
  312.3 13.2 %collective-permute-done.9 = f32[1,512,256]{2,1,0:T(8,128)S(1)} collective-permute-done((f32[1,512,256]{2,1,0:T(8,128)S(1)}, f32[1,512,256]{2,1,0:T(8,128)S(1)}, u32[]{:S(2)}, u32[]{:S(2)}) %collective-permute-start.9) | collective-permute-done | bytes 524320 | tf_op jit(solution)/shard_map/ppermute | solution.py:22
  327.3 12.9 %scatter_fusion.2 = f32[2048,256]{1,0:T(8,128)S(1)} fusion(f32[2048,256]{1,0:T(8,128)S(1)} %copy.52, s32[2048]{0:T(1024)S(1)} %bitcast.119, f32[2048,256]{1,0:T(8,128)} %bitcast_multiply_fusion.1), kind=kCustom, calls=%fused_computation.7 | custom fusion | flops 524288 | bytes 6299648 | tf_op jit(solution)/shard_map/scatter-add | solution.py:65
  342.0 70.5 %all-gather.5.cloned.1.call-done = f32[4096,256]{1,0:T(8,128)} async-done(((f32[32,256]{1,0:T(8,128)}), f32[4096,256]{1,0:T(8,128)}) %all-gather.5.cloned.1.call-update) | async-done | bytes 4194320 | tf_op jit(solution)/shard_map/all_gather | solution.py:84
  415.5 13.4 %all_to_all.10 = f32[16,32,256]{2,1,0:T(8,128)S(1)} all-to-all(f32[16,32,256]{2,1,0:T(8,128)} %bitcast.115), channel_id=1, replica_groups=mesh['row_0'=4,'row_1'=2,'col_0'=2,'col_1'=4,'col_2'=2] {'col_0','col_1'..., dimensions={0} | all-to-all | bytes 1048576 | tf_op jit(solution)/shard_map/all_to_all | solution.py:35
  435.0 10.2 %gather_fusion.3 = f32[2048,256]{1,0:T(8,128)} fusion(f32[2048,256]{1,0:T(8,128)} %copy.55, s32[2048]{0:T(1024)S(1)} %broadcast_clamp_fusion), kind=kCustom, calls=%fused_computation.3.clone | custom fusion | bytes 4202496 | tf_op jit(solution)/shard_map/jit(_take)/gather | solution.py:59
  448.3 4.5 collective-permute-start.12
  462.4 12.8 %collective-permute-done.13 = f32[1,512,256]{2,1,0:T(8,128)} collective-permute-done((f32[1,512,256]{2,1,0:T(8,128)}, f32[1,512,256]{2,1,0:T(8,128)}, u32[]{:S(2)}, u32[]{:S(2)}) %collective-permute-start.13) | collective-permute-done | bytes 524320 | tf_op jit(solution)/shard_map/ppermute | solution.py:22
  479.1 12.9 %scatter_fusion.3 = f32[2048,256]{1,0:T(8,128)S(1)} fusion(f32[2048,256]{1,0:T(8,128)S(1)} %copy-done.2, s32[2048]{0:T(1024)S(1)} %bitcast.120, f32[2048,256]{1,0:T(8,128)} %bitcast_multiply_fusion), kind=kCustom, calls=%fused_computation.8 | custom fusion | flops 524288 | bytes 6299648 | tf_op jit(solution)/shard_map/scatter-add | solution.py:65
  496.5 6.7 %fusion.28 = f32[256]{0:T(256)S(1)} fusion(f32[2048,256]{0,1:T(8,128)S(1)} %get-tuple-element.27, bf16[1,1,2048,2048]{3,2,1,0:T(8,128)(2,1)} %param.9), kind=kOutput, calls=%fused_computation.40 | convolution fusion | flops 2149056256 | bytes 10486784 | tf_op jit(solution)/shard_map/dot_general | solution.py:105
  503.2 7.0 %all-reduce.2 = (f32[256]{0:T(256)S(1)}, f32[256]{0:T(256)S(1)}) all-reduce(f32[256]{0:T(256)S(1)} %get-tuple-element.26, f32[256]{0:T(256)S(1)} %fusion.28), channel_id=1, replica_groups=mesh['row_0'=4,'row_1'=2,'col_0'=2,'col_1'=4,'col_2'=2] {'row_0'}, use_global_device_ids=true, to_apply=%region_20.22 | all-reduce | flops 512 | bytes 4096 | tf_op jit(solution)/shard_map/psum | solution.py:40
  510.2 5.3 all-reduce.8
  515.5 4.6 all-reduce.6
  520.1 14.5 %all-reduce = (f32[256]{0:T(256)S(1)}, f32[256]{0:T(256)S(1)}) all-reduce(f32[256]{0:T(256)S(1)} %get-tuple-element.18, f32[256]{0:T(256)S(1)} %get-tuple-element.19), channel_id=1, replica_groups=mesh['row_0'=4,'row_1'=2,'col_0'=2,'col_1'=4,'col_2'=2] {'col_1'}, use_global_device_ids=true, to_apply=%region_23.25 | all-reduce | flops 512 | bytes 4096 | tf_op jit(solution)/shard_map/psum | solution.py:40
  534.5 7.1 %all-reduce.4 = (f32[256]{0:T(256)S(1)}, f32[256]{0:T(256)S(1)}) all-reduce(f32[256]{0:T(256)S(1)} %get-tuple-element.6, f32[256]{0:T(256)S(1)} %get-tuple-element.7), channel_id=1, replica_groups=mesh['row_0'=4,'row_1'=2,'col_0'=2,'col_1'=4,'col_2'=2] {'col_2'}, use_global_device_ids=true, to_apply=%region_24.26 | all-reduce | flops 512 | bytes 4096 | tf_op jit(solution)/shard_map/psum | solution.py:40
  (110 shorter events, 122.9 us)
Async XLA Ops:
  6.5 138.0 %copy-start = (f32[512,256]{1,0:T(8,128)S(1)}, f32[512,256]{1,0:T(8,128)}, u32[]{:S(2)}) copy-start(f32[512,256]{1,0:T(8,128)} %param.12) | copy-start | bytes 1572868
  6.5 138.0 %all-gather.3.cloned.1.call-start = ((), (), s32[]{:S(2)}) async-start(), calls=%async_computation.2 | async-start | bytes 4227072 | tf_op jit(solution)/shard_map/all_gather | solution.py:84
  10.0 1.3 copy-start.3
  25.2 13.3 %copy-start.10 = (s32[1,1,4]{2,1,0:T(1,128)S(1)}, s32[1,1,4]{2,1,0:T(1,128)}, u32[]{:S(2)}) copy-start(s32[1,1,4]{2,1,0:T(1,128)} %param.14) | copy-start | bytes 52
  25.2 13.4 %copy-start.8 = (s32[1,1,4,512]{3,2,1,0:T(4,128)S(1)}, s32[1,1,4,512]{3,2,1,0:T(4,128)}, u32[]{:S(2)}) copy-start(s32[1,1,4,512]{3,2,1,0:T(4,128)} %param.13) | copy-start | bytes 24580
  25.4 16.1 %collective-permute-start = (f32[1,512,256]{2,1,0:T(8,128)S(1)}, f32[1,512,256]{2,1,0:T(8,128)S(1)}, u32[]{:S(2)}, u32[]{:S(2)}) collective-permute-start(f32[1,512,256]{2,1,0:T(8,128)S(1)} %get-tuple-element.42), channel_id=1, source_target_pairs={{0,16},{16,32},{32,48},{48,64},{64,80},{80,96},{96,112},{1,17},{17... | collective-permute-start | bytes 1572872 | tf_op jit(solution)/shard_map/ppermute | solution.py:19
  30.9 23.8 %collective-permute-start.1 = (f32[1,512,256]{2,1,0:T(8,128)S(1)}, f32[1,512,256]{2,1,0:T(8,128)S(1)}, u32[]{:S(2)}, u32[]{:S(2)}) collective-permute-start(f32[1,512,256]{2,1,0:T(8,128)S(1)} %get-tuple-element.45), channel_id=1, source_target_pairs={{16,0},{32,16},{48,32},{64,48},{80,64},{96,80},{112,96},{17,1},{33... | collective-permute-start | bytes 1572872 | tf_op jit(solution)/shard_map/ppermute | solution.py:22
  32.2 22.5 %collective-permute-start.2 = (f32[1,512,256]{2,1,0:T(8,128)S(1)}, f32[1,512,256]{2,1,0:T(8,128)S(1)}, u32[]{:S(2)}, u32[]{:S(2)}) collective-permute-start(f32[1,512,256]{2,1,0:T(8,128)S(1)} %get-tuple-element.44), channel_id=1, source_target_pairs={{0,1},{1,2},{2,3},{3,4},{4,5},{5,6},{6,7},{7,8},{8,9},{9,10},{10,1... | collective-permute-start | bytes 1572872 | tf_op jit(solution)/shard_map/ppermute | solution.py:19
  36.6 18.1 %collective-permute-start.3 = (f32[1,512,256]{2,1,0:T(8,128)S(1)}, f32[1,512,256]{2,1,0:T(8,128)S(1)}, u32[]{:S(2)}, u32[]{:S(2)}) collective-permute-start(f32[1,512,256]{2,1,0:T(8,128)S(1)} %get-tuple-element.43), channel_id=1, source_target_pairs={{1,0},{2,1},{3,2},{4,3},{5,4},{6,5},{7,6},{8,7},{9,8},{10,9},{11,1... | collective-permute-start | bytes 1572872 | tf_op jit(solution)/shard_map/ppermute | solution.py:22
  56.5 12.8 %copy-start.7 = (f32[1,1,32,2048]{3,2,1,0:T(8,128)S(1)}, f32[1,1,32,2048]{3,2,1,0:T(8,128)}, u32[]{:S(2)}) copy-start(f32[1,1,32,2048]{3,2,1,0:T(8,128)} %param.11) | copy-start | bytes 786436
  147.5 13.4 %all-to-all-start = ((f32[16,32,256]{2,1,0:T(8,128)}), f32[16,32,256]{2,1,0:T(8,128)S(1)}, u32[]{:S(2)}, u32[]{:S(2)}) async-start(f32[16,32,256]{2,1,0:T(8,128)} %bitcast.114), calls=%async_computation | async-start | bytes 1048576 | tf_op jit(solution)/shard_map/all_to_all | solution.py:35
  151.2 261.3 %all-gather.5.cloned.1.call-start = ((), (), s32[]{:S(2)}) async-start(), calls=%async_computation.3 | async-start | bytes 4227072 | tf_op jit(solution)/shard_map/all_gather | solution.py:84
  179.1 21.2 %copy-start.9 = (s32[1,1,2048]{2,1,0:T(1,128)S(1)}, s32[1,1,2048]{2,1,0:T(1,128)}, u32[]{:S(2)}) copy-start(s32[1,1,2048]{2,1,0:T(1,128)} %param.15) | copy-start | bytes 24580
  180.3 21.8 %collective-permute-start.4 = (f32[1,512,256]{2,1,0:T(8,128)}, f32[1,512,256]{2,1,0:T(8,128)}, u32[]{:S(2)}, u32[]{:S(2)}) collective-permute-start(f32[1,512,256]{2,1,0:T(8,128)} %get-tuple-element.38), channel_id=1, source_target_pairs={{0,16},{16,32},{32,48},{48,64},{64,80},{80,96},{96,112},{1,17},{17... | collective-permute-start | bytes 1572872 | tf_op jit(solution)/shard_map/ppermute | solution.py:19
  184.8 22.3 %collective-permute-start.5 = (f32[1,512,256]{2,1,0:T(8,128)}, f32[1,512,256]{2,1,0:T(8,128)}, u32[]{:S(2)}, u32[]{:S(2)}) collective-permute-start(f32[1,512,256]{2,1,0:T(8,128)} %get-tuple-element.41), channel_id=1, source_target_pairs={{16,0},{32,16},{48,32},{64,48},{80,64},{96,80},{112,96},{17,1},{33... | collective-permute-start | bytes 1572872 | tf_op jit(solution)/shard_map/ppermute | solution.py:22
  186.1 21.0 %collective-permute-start.6 = (f32[1,512,256]{2,1,0:T(8,128)}, f32[1,512,256]{2,1,0:T(8,128)}, u32[]{:S(2)}, u32[]{:S(2)}) collective-permute-start(f32[1,512,256]{2,1,0:T(8,128)} %get-tuple-element.40), channel_id=1, source_target_pairs={{0,1},{1,2},{2,3},{3,4},{4,5},{5,6},{6,7},{7,8},{8,9},{9,10},{10,1... | collective-permute-start | bytes 1572872 | tf_op jit(solution)/shard_map/ppermute | solution.py:19
  188.0 19.1 %collective-permute-start.7 = (f32[1,512,256]{2,1,0:T(8,128)S(1)}, f32[1,512,256]{2,1,0:T(8,128)}, u32[]{:S(2)}, u32[]{:S(2)}) collective-permute-start(f32[1,512,256]{2,1,0:T(8,128)S(1)} %get-tuple-element.39), channel_id=1, source_target_pairs={{1,0},{2,1},{3,2},{4,3},{5,4},{6,5},{7,6},{8,7},{9,8},{10,9},{11,1... | collective-permute-start | bytes 1572872 | tf_op jit(solution)/shard_map/ppermute | solution.py:22
  208.8 2.3 copy-start.1
  228.3 6.7 %copy-start.5 = (f32[2048,256]{0,1:T(8,128)}, f32[2048,256]{0,1:T(8,128)S(1)}, u32[]{:S(2)}) copy-start(f32[2048,256]{0,1:T(8,128)S(1)} %get-tuple-element.29) | copy-start | bytes 6291460
  228.3 45.2 %copy-start.4 = (f32[1,1,2048,256]{2,3,1,0:T(8,128)S(1)}, f32[1,1,2048,256]{2,3,1,0:T(8,128)}, u32[]{:S(2)}) copy-start(f32[1,1,2048,256]{2,3,1,0:T(8,128)} %copy-done.3) | copy-start | bytes 6291460
  293.8 10.0 %collective-permute-start.10 = (f32[1,512,256]{2,1,0:T(8,128)S(1)}, f32[1,512,256]{2,1,0:T(8,128)S(1)}, u32[]{:S(2)}, u32[]{:S(2)}) collective-permute-start(f32[1,512,256]{2,1,0:T(8,128)S(1)} %get-tuple-element.36), channel_id=1, source_target_pairs={{0,1},{1,2},{2,3},{3,4},{4,5},{5,6},{6,7},{7,8},{8,9},{9,10},{10,1... | collective-permute-start | bytes 1572872 | tf_op jit(solution)/shard_map/ppermute | solution.py:19
  297.7 10.5 %collective-permute-start.11 = (f32[1,512,256]{2,1,0:T(8,128)S(1)}, f32[1,512,256]{2,1,0:T(8,128)S(1)}, u32[]{:S(2)}, u32[]{:S(2)}) collective-permute-start(f32[1,512,256]{2,1,0:T(8,128)S(1)} %get-tuple-element.35), channel_id=1, source_target_pairs={{1,0},{2,1},{3,2},{4,3},{5,4},{6,5},{7,6},{8,7},{9,8},{10,9},{11,1... | collective-permute-start | bytes 1572872 | tf_op jit(solution)/shard_map/ppermute | solution.py:22
  299.6 12.7 %collective-permute-start.8 = (f32[1,512,256]{2,1,0:T(8,128)S(1)}, f32[1,512,256]{2,1,0:T(8,128)S(1)}, u32[]{:S(2)}, u32[]{:S(2)}) collective-permute-start(f32[1,512,256]{2,1,0:T(8,128)S(1)} %get-tuple-element.34), channel_id=1, source_target_pairs={{0,16},{16,32},{32,48},{48,64},{64,80},{80,96},{96,112},{1,17},{17... | collective-permute-start | bytes 1572872 | tf_op jit(solution)/shard_map/ppermute | solution.py:19
  302.2 23.3 %collective-permute-start.9 = (f32[1,512,256]{2,1,0:T(8,128)S(1)}, f32[1,512,256]{2,1,0:T(8,128)S(1)}, u32[]{:S(2)}, u32[]{:S(2)}) collective-permute-start(f32[1,512,256]{2,1,0:T(8,128)S(1)} %get-tuple-element.37), channel_id=1, source_target_pairs={{16,0},{32,16},{48,32},{64,48},{80,64},{96,80},{112,96},{17,1},{33... | collective-permute-start | bytes 1572872 | tf_op jit(solution)/shard_map/ppermute | solution.py:22
  448.3 14.1 %collective-permute-start.12 = (f32[1,512,256]{2,1,0:T(8,128)}, f32[1,512,256]{2,1,0:T(8,128)}, u32[]{:S(2)}, u32[]{:S(2)}) collective-permute-start(f32[1,512,256]{2,1,0:T(8,128)} %get-tuple-element.30), channel_id=1, source_target_pairs={{0,16},{16,32},{32,48},{48,64},{64,80},{80,96},{96,112},{1,17},{17... | collective-permute-start | bytes 1572872 | tf_op jit(solution)/shard_map/ppermute | solution.py:19
  452.8 22.3 %collective-permute-start.13 = (f32[1,512,256]{2,1,0:T(8,128)}, f32[1,512,256]{2,1,0:T(8,128)}, u32[]{:S(2)}, u32[]{:S(2)}) collective-permute-start(f32[1,512,256]{2,1,0:T(8,128)} %get-tuple-element.33), channel_id=1, source_target_pairs={{16,0},{32,16},{48,32},{64,48},{80,64},{96,80},{112,96},{17,1},{33... | collective-permute-start | bytes 1572872 | tf_op jit(solution)/shard_map/ppermute | solution.py:22
  454.1 21.0 %collective-permute-start.14 = (f32[1,512,256]{2,1,0:T(8,128)}, f32[1,512,256]{2,1,0:T(8,128)}, u32[]{:S(2)}, u32[]{:S(2)}) collective-permute-start(f32[1,512,256]{2,1,0:T(8,128)} %get-tuple-element.32), channel_id=1, source_target_pairs={{0,1},{1,2},{2,3},{3,4},{4,5},{5,6},{6,7},{7,8},{8,9},{9,10},{10,1... | collective-permute-start | bytes 1572872 | tf_op jit(solution)/shard_map/ppermute | solution.py:19
  456.1 19.1 %collective-permute-start.15 = (f32[1,512,256]{2,1,0:T(8,128)S(1)}, f32[1,512,256]{2,1,0:T(8,128)}, u32[]{:S(2)}, u32[]{:S(2)}) collective-permute-start(f32[1,512,256]{2,1,0:T(8,128)S(1)} %get-tuple-element.31), channel_id=1, source_target_pairs={{1,0},{2,1},{3,2},{4,3},{5,4},{6,5},{7,6},{8,7},{9,8},{10,9},{11,1... | collective-permute-start | bytes 1572872 | tf_op jit(solution)/shard_map/ppermute | solution.py:22
  476.8 2.3 copy-start.2
  496.5 6.7 %copy-start.6 = (f32[2048,256]{0,1:T(8,128)}, f32[2048,256]{0,1:T(8,128)S(1)}, u32[]{:S(2)}) copy-start(f32[2048,256]{0,1:T(8,128)S(1)} %get-tuple-element.27) | copy-start | bytes 6291460
Sparse Core Ops, SparseCore 0:
  71.2 73.2 all-gather.2
  342.1 70.3 all-gather.4
where the time goes:
time: 563 us; the launch traced here: 554 us
  waiting for transfers between devices  210 us (37%)
  blocking collectives  90.3 us (16%)
  other arithmetic  80.6 us (14%)
  local copies, waits for them, and re-layouts  74.2 us (13%)
  starting transfers between devices  49.1 us (9%)
  matrix products  35 us (6%)
  between operations  14.1 us (3%)
    all_gather x2, waiting for transfers between devices, per_device(): gathered = lax.all_gather(coarse_coef, ROW_COL, axis=0, tiled=True)  144 us
    psum x10, blocking collectives, by_axis(): return functools.reduce(lax.psum, axes, value)  76.9 us
    scatter-add x4, other arithmetic, assemble(): return field_values.at[flat_rows].add(incoming.reshape(-1, case_count))  51.3 us
    ppermute x8, waiting for transfers between devices, extended(): lax.ppermute(lax.slice_in_dim(block, 0, width, axis=dim), axis, backward)  48.5 us
    gather x4, local copies, waits for them, and re-layouts, assemble(): blocks = jnp.take(field_values, row_index, axis=0)  37.5 us
    ppermute x8, starting transfers between devices, extended(): lax.ppermute(lax.slice_in_dim(block, block.shape[dim] - width, None, axis...  29.2 us
    ppermute x8, starting transfers between devices, extended(): lax.ppermute(lax.slice_in_dim(block, 0, width, axis=dim), axis, backward)  16.2 us
    all_to_all x1, blocking collectives, summed_on_arrival(): lax.all_to_all(blocks, axis, split_axis=0, concat_axis=0, tiled=True)  13.4 us
  transfers between devices with their start and end apart: 19, of which 12 were waited for; matrix products, arithmetic and copies ran while one was open for 2% of the time, Pallas kernels for 0%

commit v1 on v0

--- a/solution.py
+++ b/solution.py
@@ -81,7 +81,9 @@
         )
         tile_cols = coarse_inverse.shape[1]
         col_index = lax.axis_index(COL)
-        gathered = lax.all_gather(coarse_coef, ROW_COL, axis=0, tiled=True)
+        gathered = jnp.concatenate(
+            lax.all_to_all(jnp.stack([coarse_coef] * lax.axis_size(ROW_COL)), ROW_COL, 0, 0), axis=0
+        )
         coarse_block = lax.dynamic_slice_in_dim(gathered, col_index * tile_cols, tile_cols, 0)
         coarse_amount = summed_on_arrival(
             jnp.dot(

time: 563 us -> 534 us (0.948)
  waiting for transfers between devices: 210 us -> 117 us
  blocking collectives: 90.3 us -> 150 us
  starting transfers between devices: 49.1 us -> 67.2 us
  between operations: 14.1 us -> 0.71 us
    all_gather x2 -> x0, waiting for transfers between devices: 144 us -> none  [per_device(): gathered = lax.all_gather(coarse_coef, ROW_COL, axis=0, tiled=True)]
    all_to_all x0 -> x1, blocking collectives: none -> 63 us  [per_device(): lax.all_to_all(jnp.stack([coarse_coef] * lax.axis_size(ROW_COL)), ROW_COL...]
    all_to_all x0 -> x1, waiting for transfers between devices: none -> 52.2 us  [per_device(): lax.all_to_all(jnp.stack([coarse_coef] * lax.axis_size(ROW_COL)), ROW_COL...]
    all_to_all x0 -> x1, starting transfers between devices: none -> 16.7 us  [per_device(): lax.all_to_all(jnp.stack([coarse_coef] * lax.axis_size(ROW_COL)), ROW_COL...]
  transfers between devices with their start and end apart: 19 -> 18, of which waited for: 12 -> 15; matrix products, arithmetic and copies ran while one was open for 2% -> 2% of each run, Pallas kernels for 0% -> 0%
where the time goes in v1:
time: 534 us; the launch traced here: 524 us
  blocking collectives  150 us (28%)
  waiting for transfers between devices  117 us (22%)
  other arithmetic  80.6 us (15%)
  local copies, waits for them, and re-layouts  76.6 us (14%)
  starting transfers between devices  67.2 us (13%)
  matrix products  32.8 us (6%)
    psum x10, blocking collectives, by_axis(): return functools.reduce(lax.psum, axes, value)  72.3 us
    all_to_all x1, blocking collectives, per_device(): lax.all_to_all(jnp.stack([coarse_coef] * lax.axis_size(ROW_COL)), ROW_COL...  63 us
    all_to_all x1, waiting for transfers between devices, per_device(): lax.all_to_all(jnp.stack([coarse_coef] * lax.axis_size(ROW_COL)), ROW_COL...  52.2 us
    scatter-add x4, other arithmetic, assemble(): return field_values.at[flat_rows].add(incoming.reshape(-1, case_count))  51.3 us
    ppermute x8, waiting for transfers between devices, extended(): lax.ppermute(lax.slice_in_dim(block, 0, width, axis=dim), axis, backward)  43.9 us
    gather x4, local copies, waits for them, and re-layouts, assemble(): blocks = jnp.take(field_values, row_index, axis=0)  37.5 us
    ppermute x8, starting transfers between devices, extended(): lax.ppermute(lax.slice_in_dim(block, block.shape[dim] - width, None, axis...  27.7 us
    ppermute x8, starting transfers between devices, extended(): lax.ppermute(lax.slice_in_dim(block, 0, width, axis=dim), axis, backward)  17.9 us
  transfers between devices with their start and end apart: 18, of which 15 were waited for; matrix products, arithmetic and copies ran while one was open for 2% of the time, Pallas kernels for 0%

profile of v1, /device:TPU:1, one launch (start us, length us, event | category | flops | bytes accessed | tf_op | source)
XLA Modules:
  0.0 524.3 jit_solution(2476453764260091207)
XLA Ops:
  8.2 8.6 %gather_fusion = f32[2048,256]{1,0:T(8,128)} fusion(f32[2048,256]{1,0:T(8,128)S(1)} %copy.29, s32[2048]{0:T(1024)S(1)} %broadcast_clamp_fusion), kind=kCustom, calls=%fused_computation.clone | custom fusion | bytes 4202496 | tf_op jit(solution)/shard_map/jit(_take)/gather | solution.py:59
  18.8 5.5 %collective-permute-start = (f32[1,512,256]{2,1,0:T(8,128)S(1)}, f32[1,512,256]{2,1,0:T(8,128)S(1)}, u32[]{:S(2)}, u32[]{:S(2)}) collective-permute-start(f32[1,512,256]{2,1,0:T(8,128)S(1)} %get-tuple-element.42), channel_id=1, source_target_pairs={{0,16},{16,32},{32,48},{48,64},{64,80},{80,96},{96,112},{1,17},{17... | collective-permute-start | bytes 1572872 | tf_op jit(solution)/shard_map/ppermute | solution.py:19
  36.8 11.3 %collective-permute-done.1 = f32[1,512,256]{2,1,0:T(8,128)S(1)} collective-permute-done((f32[1,512,256]{2,1,0:T(8,128)S(1)}, f32[1,512,256]{2,1,0:T(8,128)S(1)}, u32[]{:S(2)}, u32[]{:S(2)}) %collective-permute-start.1) | collective-permute-done | bytes 524320 | tf_op jit(solution)/shard_map/ppermute | solution.py:22
  49.9 12.7 %scatter_fusion = f32[2048,256]{1,0:T(8,128)S(1)} fusion(f32[2048,256]{1,0:T(8,128)S(1)} %copy.29, s32[2048]{0:T(1024)S(1)} %bitcast.120, f32[2048,256]{1,0:T(8,128)} %bitcast_multiply_fusion.3), kind=kCustom, calls=%fused_computation.5 | custom fusion | flops 524288 | bytes 6299648 | tf_op jit(solution)/shard_map/scatter-add | solution.py:65
  66.4 16.7 %all-to-all-start = ((f32[128,32,256]{2,1,0:T(8,128)}), f32[128,32,256]{2,1,0:T(8,128)}, u32[]{:S(2)}, u32[]{:S(2)}) async-start(f32[128,32,256]{2,1,0:T(8,128)} %stack.22), calls=%async_computation | async-start | bytes 8388608 | tf_op jit(solution)/shard_map/all_to_all | solution.py:85
  83.1 52.2 %all-to-all-done = f32[128,32,256]{2,1,0:T(8,128)} async-done(((f32[128,32,256]{2,1,0:T(8,128)}), f32[128,32,256]{2,1,0:T(8,128)}, u32[]{:S(2)}, u32[]{:S(2)}) %all-to-all-start) | async-done | bytes 4194336 | tf_op jit(solution)/shard_map/all_to_all | solution.py:85
  138.4 4.8 all-to-all-start.1
  143.1 9.7 %all-to-all-done.1 = f32[16,32,256]{2,1,0:T(8,128)S(1)} async-done(((f32[16,32,256]{2,1,0:T(8,128)}), f32[16,32,256]{2,1,0:T(8,128)S(1)}, u32[]{:S(2)}, u32[]{:S(2)}) %all-to-all-start.1) | async-done | bytes 524320 | tf_op jit(solution)/shard_map/all_to_all | solution.py:35
  159.0 10.1 %gather_fusion.1 = f32[2048,256]{1,0:T(8,128)} fusion(f32[2048,256]{1,0:T(8,128)} %copy.32, s32[2048]{0:T(1024)S(1)} %broadcast_clamp_fusion), kind=kCustom, calls=%fused_computation.1.clone | custom fusion | bytes 4202496 | tf_op jit(solution)/shard_map/jit(_take)/gather | solution.py:59
  183.1 8.0 %scatter_custom_fusion = f32[2048]{0:T(1024)S(1)} fusion(s32[2048]{0:T(1024)S(1)} %bitcast.121, f32[2048]{0:T(1024)S(1)} %bitcast.132, f32[]{:T(128)} %constant.19.clone.1), kind=kCustom, calls=%fused_computation.70 | custom fusion | bytes 8196 | tf_op jit(solution)/shard_map/scatter | solution.py:54
  193.0 6.2 %collective-permute-done.5 = f32[1,512,256]{2,1,0:T(8,128)} collective-permute-done((f32[1,512,256]{2,1,0:T(8,128)S(1)}, f32[1,512,256]{2,1,0:T(8,128)}, u32[]{:S(2)}, u32[]{:S(2)}) %collective-permute-start.5) | collective-permute-done | bytes 524320 | tf_op jit(solution)/shard_map/ppermute | solution.py:22
  203.2 12.7 %scatter_fusion.1 = f32[2048,256]{1,0:T(8,128)S(1)} fusion(f32[2048,256]{1,0:T(8,128)S(1)} %copy-done.1, s32[2048]{0:T(1024)S(1)} %bitcast.122, f32[2048,256]{1,0:T(8,128)} %bitcast_multiply_fusion.2), kind=kCustom, calls=%fused_computation.6 | custom fusion | flops 524288 | bytes 6299648 | tf_op jit(solution)/shard_map/scatter-add | solution.py:65
  220.4 6.7 %fusion.31 = f32[256]{0:T(256)S(1)} fusion(f32[2048,256]{0,1:T(8,128)S(1)} %get-tuple-element.29, bf16[1,1,2048,2048]{3,2,1,0:T(8,128)(2,1)} %param.9), kind=kOutput, calls=%fused_computation.41 | convolution fusion | flops 2149056256 | bytes 10486784 | tf_op jit(solution)/shard_map/dot_general | solution.py:107
  227.1 6.0 %all-reduce.3 = (f32[256]{0:T(256)S(1)}, f32[256]{0:T(256)S(1)}) all-reduce(f32[256]{0:T(256)S(1)} %get-tuple-element.28, f32[256]{0:T(256)S(1)} %fusion.31), channel_id=1, replica_groups=mesh['row_0'=4,'row_1'=2,'col_0'=2,'col_1'=4,'col_2'=2] {'row_0'}, use_global_device_ids=true, to_apply=%region_5.7 | all-reduce | flops 512 | bytes 4096 | tf_op jit(solution)/shard_map/psum | solution.py:40
  233.1 5.3 %all-reduce.9 = (f32[256]{0:T(256)S(1)}, f32[256]{0:T(256)S(1)}) all-reduce(f32[256]{0:T(256)S(1)} %get-tuple-element.12, f32[256]{0:T(256)S(1)} %get-tuple-element.13), channel_id=1, replica_groups=mesh['row_0'=4,'row_1'=2,'col_0'=2,'col_1'=4,'col_2'=2] {'row_1'}, use_global_device_ids=true, to_apply=%region_6.8 | all-reduce | flops 512 | bytes 4096 | tf_op jit(solution)/shard_map/psum | solution.py:40
  238.4 4.4 all-reduce.7
  242.8 14.1 %all-reduce.1 = (f32[256]{0:T(256)S(1)}, f32[256]{0:T(256)S(1)}) all-reduce(f32[256]{0:T(256)S(1)} %get-tuple-element.20, f32[256]{0:T(256)S(1)} %get-tuple-element.21), channel_id=1, replica_groups=mesh['row_0'=4,'row_1'=2,'col_0'=2,'col_1'=4,'col_2'=2] {'col_1'}, use_global_device_ids=true, to_apply=%region_8.10 | all-reduce | flops 512 | bytes 4096 | tf_op jit(solution)/shard_map/psum | solution.py:40
  256.9 6.4 %all-reduce.5 = (f32[256]{0:T(256)S(1)}, f32[256]{0:T(256)S(1)}) all-reduce(f32[256]{0:T(256)S(1)} %get-tuple-element.8, f32[256]{0:T(256)S(1)} %get-tuple-element.9), channel_id=1, replica_groups=mesh['row_0'=4,'row_1'=2,'col_0'=2,'col_1'=4,'col_2'=2] {'col_2'}, use_global_device_ids=true, to_apply=%region_9.11 | all-reduce | flops 512 | bytes 4096 | tf_op jit(solution)/shard_map/psum | solution.py:40
  263.3 7.7 %fusion.21 = f32[2048,256]{0,1:T(8,128)} fusion(bf16[1,1,2048,2048]{3,2,1,0:T(8,128)(2,1)} %param.9, f32[1,1,2048,256]{2,3,1,0:T(8,128)S(1)} %copy-done.4, f32[2048,256]{0,1:T(8,128)} %copy-done.5, f32[256]{0:T(256)S(1)} %div.6, pred[2048]{0:T(1024)(128)(4,1)S(1)} %multiply_compare_fusion), kind=kOutput, calls=%fused_computation.26 | convolution fusion | flops 2150629376 | bytes 14683136 | tf_op jit(solution)/shard_map/dot_general | solution.py:73
  272.9 8.6 %gather_fusion.2 = f32[2048,256]{1,0:T(8,128)} fusion(f32[2048,256]{1,0:T(8,128)S(1)} %copy.36, s32[2048]{0:T(1024)S(1)} %broadcast_clamp_fusion), kind=kCustom, calls=%fused_computation.2.clone | custom fusion | bytes 4202496 | tf_op jit(solution)/shard_map/jit(_take)/gather | solution.py:59
  300.1 12.6 %collective-permute-done.9 = f32[1,512,256]{2,1,0:T(8,128)S(1)} collective-permute-done((f32[1,512,256]{2,1,0:T(8,128)S(1)}, f32[1,512,256]{2,1,0:T(8,128)S(1)}, u32[]{:S(2)}, u32[]{:S(2)}) %collective-permute-start.9) | collective-permute-done | bytes 524320 | tf_op jit(solution)/shard_map/ppermute | solution.py:22
  314.5 12.9 %scatter_fusion.2 = f32[2048,256]{1,0:T(8,128)S(1)} fusion(f32[2048,256]{1,0:T(8,128)S(1)} %copy.36, s32[2048]{0:T(1024)S(1)} %bitcast.123, f32[2048,256]{1,0:T(8,128)} %bitcast_multiply_fusion.1), kind=kCustom, calls=%fused_computation.7 | custom fusion | flops 524288 | bytes 6299648 | tf_op jit(solution)/shard_map/scatter-add | solution.py:65
  329.1 63.0 %all_to_all.20 = f32[128,32,256]{2,1,0:T(8,128)S(1)} all-to-all(f32[128,32,256]{2,1,0:T(8,128)S(1)} %stack.27), channel_id=1, replica_groups=mesh['row_0'=4,'row_1'=2,'col_0'=2,'col_1'=4,'col_2'=2] {'row_0','row_1'..., dimensions={0} | all-to-all | bytes 8388608 | tf_op jit(solution)/shard_map/all_to_all | solution.py:85
  394.2 14.5 %all_to_all.21 = f32[16,32,256]{2,1,0:T(8,128)S(1)} all-to-all(f32[16,32,256]{2,1,0:T(8,128)} %bitcast.119), channel_id=1, replica_groups=mesh['row_0'=4,'row_1'=2,'col_0'=2,'col_1'=4,'col_2'=2] {'col_0','col_1'..., dimensions={0} | all-to-all | bytes 1048576 | tf_op jit(solution)/shard_map/all_to_all | solution.py:35
  414.8 10.2 %gather_fusion.3 = f32[2048,256]{1,0:T(8,128)} fusion(f32[2048,256]{1,0:T(8,128)} %copy.39, s32[2048]{0:T(1024)S(1)} %broadcast_clamp_fusion), kind=kCustom, calls=%fused_computation.3.clone | custom fusion | bytes 4202496 | tf_op jit(solution)/shard_map/jit(_take)/gather | solution.py:59
  443.5 11.6 %collective-permute-done.13 = f32[1,512,256]{2,1,0:T(8,128)} collective-permute-done((f32[1,512,256]{2,1,0:T(8,128)S(1)}, f32[1,512,256]{2,1,0:T(8,128)}, u32[]{:S(2)}, u32[]{:S(2)}) %collective-permute-start.13) | collective-permute-done | bytes 524320 | tf_op jit(solution)/shard_map/ppermute | solution.py:22
  459.0 12.9 %scatter_fusion.3 = f32[2048,256]{1,0:T(8,128)S(1)} fusion(f32[2048,256]{1,0:T(8,128)S(1)} %copy-done.2, s32[2048]{0:T(1024)S(1)} %bitcast.124, f32[2048,256]{1,0:T(8,128)} %bitcast_multiply_fusion), kind=kCustom, calls=%fused_computation.8 | custom fusion | flops 524288 | bytes 6299648 | tf_op jit(solution)/shard_map/scatter-add | solution.py:65
  476.4 6.7 %fusion.28 = f32[256]{0:T(256)S(1)} fusion(f32[2048,256]{0,1:T(8,128)S(1)} %get-tuple-element.27, bf16[1,1,2048,2048]{3,2,1,0:T(8,128)(2,1)} %param.9), kind=kOutput, calls=%fused_computation.40 | convolution fusion | flops 2149056256 | bytes 10486784 | tf_op jit(solution)/shard_map/dot_general | solution.py:107
  483.1 6.0 %all-reduce.2 = (f32[256]{0:T(256)S(1)}, f32[256]{0:T(256)S(1)}) all-reduce(f32[256]{0:T(256)S(1)} %get-tuple-element.26, f32[256]{0:T(256)S(1)} %fusion.28), channel_id=1, replica_groups=mesh['row_0'=4,'row_1'=2,'col_0'=2,'col_1'=4,'col_2'=2] {'row_0'}, use_global_device_ids=true, to_apply=%region_20.22 | all-reduce | flops 512 | bytes 4096 | tf_op jit(solution)/shard_map/psum | solution.py:40
  489.1 5.3 %all-reduce.8 = (f32[256]{0:T(256)S(1)}, f32[256]{0:T(256)S(1)}) all-reduce(f32[256]{0:T(256)S(1)} %get-tuple-element.10, f32[256]{0:T(256)S(1)} %get-tuple-element.11), channel_id=1, replica_groups=mesh['row_0'=4,'row_1'=2,'col_0'=2,'col_1'=4,'col_2'=2] {'row_1'}, use_global_device_ids=true, to_apply=%region_21.23 | all-reduce | flops 512 | bytes 4096 | tf_op jit(solution)/shard_map/psum | solution.py:40
  498.8 14.1 %all-reduce = (f32[256]{0:T(256)S(1)}, f32[256]{0:T(256)S(1)}) all-reduce(f32[256]{0:T(256)S(1)} %get-tuple-element.18, f32[256]{0:T(256)S(1)} %get-tuple-element.19), channel_id=1, replica_groups=mesh['row_0'=4,'row_1'=2,'col_0'=2,'col_1'=4,'col_2'=2] {'col_1'}, use_global_device_ids=true, to_apply=%region_23.25 | all-reduce | flops 512 | bytes 4096 | tf_op jit(solution)/shard_map/psum | solution.py:40
  512.9 6.4 %all-reduce.4 = (f32[256]{0:T(256)S(1)}, f32[256]{0:T(256)S(1)}) all-reduce(f32[256]{0:T(256)S(1)} %get-tuple-element.6, f32[256]{0:T(256)S(1)} %get-tuple-element.7), channel_id=1, replica_groups=mesh['row_0'=4,'row_1'=2,'col_0'=2,'col_1'=4,'col_2'=2] {'col_2'}, use_global_device_ids=true, to_apply=%region_24.26 | all-reduce | flops 512 | bytes 4096 | tf_op jit(solution)/shard_map/psum | solution.py:40
  (109 shorter events, 129.4 us)
Async XLA Ops:
  0.0 135.4 %copy-start = (f32[512,256]{1,0:T(8,128)S(1)}, f32[512,256]{1,0:T(8,128)}, u32[]{:S(2)}) copy-start(f32[512,256]{1,0:T(8,128)} %param.12) | copy-start | bytes 1572868
  3.4 1.3 copy-start.3
  18.7 13.3 %copy-start.10 = (s32[1,1,4]{2,1,0:T(1,128)S(1)}, s32[1,1,4]{2,1,0:T(1,128)}, u32[]{:S(2)}) copy-start(s32[1,1,4]{2,1,0:T(1,128)} %param.14) | copy-start | bytes 52
  18.7 13.4 %copy-start.8 = (s32[1,1,4,512]{3,2,1,0:T(4,128)S(1)}, s32[1,1,4,512]{3,2,1,0:T(4,128)}, u32[]{:S(2)}) copy-start(s32[1,1,4,512]{3,2,1,0:T(4,128)} %param.13) | copy-start | bytes 24580
  18.8 16.1 %collective-permute-start = (f32[1,512,256]{2,1,0:T(8,128)S(1)}, f32[1,512,256]{2,1,0:T(8,128)S(1)}, u32[]{:S(2)}, u32[]{:S(2)}) collective-permute-start(f32[1,512,256]{2,1,0:T(8,128)S(1)} %get-tuple-element.42), channel_id=1, source_target_pairs={{0,16},{16,32},{32,48},{48,64},{64,80},{80,96},{96,112},{1,17},{17... | collective-permute-start | bytes 1572872 | tf_op jit(solution)/shard_map/ppermute | solution.py:19
  24.3 11.2 %collective-permute-start.3 = (f32[1,512,256]{2,1,0:T(8,128)S(1)}, f32[1,512,256]{2,1,0:T(8,128)S(1)}, u32[]{:S(2)}, u32[]{:S(2)}) collective-permute-start(f32[1,512,256]{2,1,0:T(8,128)S(1)} %get-tuple-element.43), channel_id=1, source_target_pairs={{1,0},{2,1},{3,2},{4,3},{5,4},{6,5},{7,6},{8,7},{9,8},{10,9},{11,1... | collective-permute-start | bytes 1572872 | tf_op jit(solution)/shard_map/ppermute | solution.py:22
  27.2 9.6 %collective-permute-start.2 = (f32[1,512,256]{2,1,0:T(8,128)S(1)}, f32[1,512,256]{2,1,0:T(8,128)S(1)}, u32[]{:S(2)}, u32[]{:S(2)}) collective-permute-start(f32[1,512,256]{2,1,0:T(8,128)S(1)} %get-tuple-element.44), channel_id=1, source_target_pairs={{0,1},{1,2},{2,3},{3,4},{4,5},{5,6},{6,7},{7,8},{8,9},{9,10},{10,1... | collective-permute-start | bytes 1572872 | tf_op jit(solution)/shard_map/ppermute | solution.py:19
  30.7 17.4 %collective-permute-start.1 = (f32[1,512,256]{2,1,0:T(8,128)S(1)}, f32[1,512,256]{2,1,0:T(8,128)S(1)}, u32[]{:S(2)}, u32[]{:S(2)}) collective-permute-start(f32[1,512,256]{2,1,0:T(8,128)S(1)} %get-tuple-element.45), channel_id=1, source_target_pairs={{16,0},{32,16},{48,32},{64,48},{80,64},{96,80},{112,96},{17,1},{33... | collective-permute-start | bytes 1572872 | tf_op jit(solution)/shard_map/ppermute | solution.py:22
  49.9 12.8 %copy-start.7 = (f32[1,1,32,2048]{3,2,1,0:T(8,128)S(1)}, f32[1,1,32,2048]{3,2,1,0:T(8,128)}, u32[]{:S(2)}) copy-start(f32[1,1,32,2048]{3,2,1,0:T(8,128)} %param.11) | copy-start | bytes 786436
  66.4 69.0 %all-to-all-start = ((f32[128,32,256]{2,1,0:T(8,128)}), f32[128,32,256]{2,1,0:T(8,128)}, u32[]{:S(2)}, u32[]{:S(2)}) async-start(f32[128,32,256]{2,1,0:T(8,128)} %stack.22), calls=%async_computation | async-start | bytes 8388608 | tf_op jit(solution)/shard_map/all_to_all | solution.py:85
  138.4 14.5 %all-to-all-start.1 = ((f32[16,32,256]{2,1,0:T(8,128)}), f32[16,32,256]{2,1,0:T(8,128)S(1)}, u32[]{:S(2)}, u32[]{:S(2)}) async-start(f32[16,32,256]{2,1,0:T(8,128)} %bitcast.118), calls=%async_computation.1 | async-start | bytes 1048576 | tf_op jit(solution)/shard_map/all_to_all | solution.py:35
  171.1 12.0 %copy-start.9 = (s32[1,1,2048]{2,1,0:T(1,128)S(1)}, s32[1,1,2048]{2,1,0:T(1,128)}, u32[]{:S(2)}) copy-start(s32[1,1,2048]{2,1,0:T(1,128)} %param.15) | copy-start | bytes 24580
  172.3 20.7 %collective-permute-start.4 = (f32[1,512,256]{2,1,0:T(8,128)}, f32[1,512,256]{2,1,0:T(8,128)}, u32[]{:S(2)}, u32[]{:S(2)}) collective-permute-start(f32[1,512,256]{2,1,0:T(8,128)} %get-tuple-element.38), channel_id=1, source_target_pairs={{0,16},{16,32},{32,48},{48,64},{64,80},{80,96},{96,112},{1,17},{17... | collective-permute-start | bytes 1572872 | tf_op jit(solution)/shard_map/ppermute | solution.py:19
  175.7 17.3 %collective-permute-start.7 = (f32[1,512,256]{2,1,0:T(8,128)}, f32[1,512,256]{2,1,0:T(8,128)}, u32[]{:S(2)}, u32[]{:S(2)}) collective-permute-start(f32[1,512,256]{2,1,0:T(8,128)} %get-tuple-element.39), channel_id=1, source_target_pairs={{1,0},{2,1},{3,2},{4,3},{5,4},{6,5},{7,6},{8,7},{9,8},{10,9},{11,1... | collective-permute-start | bytes 1572872 | tf_op jit(solution)/shard_map/ppermute | solution.py:22
  179.1 13.9 %collective-permute-start.6 = (f32[1,512,256]{2,1,0:T(8,128)}, f32[1,512,256]{2,1,0:T(8,128)}, u32[]{:S(2)}, u32[]{:S(2)}) collective-permute-start(f32[1,512,256]{2,1,0:T(8,128)} %get-tuple-element.40), channel_id=1, source_target_pairs={{0,1},{1,2},{2,3},{3,4},{4,5},{5,6},{6,7},{7,8},{8,9},{9,10},{10,1... | collective-permute-start | bytes 1572872 | tf_op jit(solution)/shard_map/ppermute | solution.py:19
  181.2 18.0 %collective-permute-start.5 = (f32[1,512,256]{2,1,0:T(8,128)S(1)}, f32[1,512,256]{2,1,0:T(8,128)}, u32[]{:S(2)}, u32[]{:S(2)}) collective-permute-start(f32[1,512,256]{2,1,0:T(8,128)S(1)} %get-tuple-element.41), channel_id=1, source_target_pairs={{16,0},{32,16},{48,32},{64,48},{80,64},{96,80},{112,96},{17,1},{33... | collective-permute-start | bytes 1572872 | tf_op jit(solution)/shard_map/ppermute | solution.py:22
  200.9 2.3 copy-start.1
  220.4 6.7 %copy-start.5 = (f32[2048,256]{0,1:T(8,128)}, f32[2048,256]{0,1:T(8,128)S(1)}, u32[]{:S(2)}) copy-start(f32[2048,256]{0,1:T(8,128)S(1)} %get-tuple-element.29) | copy-start | bytes 6291460
  220.4 42.9 %copy-start.4 = (f32[1,1,2048,256]{2,3,1,0:T(8,128)S(1)}, f32[1,1,2048,256]{2,3,1,0:T(8,128)}, u32[]{:S(2)}) copy-start(f32[1,1,2048,256]{2,3,1,0:T(8,128)} %copy-done.3) | copy-start | bytes 6291460
  283.6 15.1 %collective-permute-start.8 = (f32[1,512,256]{2,1,0:T(8,128)S(1)}, f32[1,512,256]{2,1,0:T(8,128)S(1)}, u32[]{:S(2)}, u32[]{:S(2)}) collective-permute-start(f32[1,512,256]{2,1,0:T(8,128)S(1)} %get-tuple-element.34), channel_id=1, source_target_pairs={{0,16},{16,32},{32,48},{48,64},{64,80},{80,96},{96,112},{1,17},{17... | collective-permute-start | bytes 1572872 | tf_op jit(solution)/shard_map/ppermute | solution.py:19
  287.9 11.0 %collective-permute-start.11 = (f32[1,512,256]{2,1,0:T(8,128)S(1)}, f32[1,512,256]{2,1,0:T(8,128)S(1)}, u32[]{:S(2)}, u32[]{:S(2)}) collective-permute-start(f32[1,512,256]{2,1,0:T(8,128)S(1)} %get-tuple-element.35), channel_id=1, source_target_pairs={{1,0},{2,1},{3,2},{4,3},{5,4},{6,5},{7,6},{8,7},{9,8},{10,9},{11,1... | collective-permute-start | bytes 1572872 | tf_op jit(solution)/shard_map/ppermute | solution.py:22
  290.4 9.6 %collective-permute-start.10 = (f32[1,512,256]{2,1,0:T(8,128)S(1)}, f32[1,512,256]{2,1,0:T(8,128)S(1)}, u32[]{:S(2)}, u32[]{:S(2)}) collective-permute-start(f32[1,512,256]{2,1,0:T(8,128)S(1)} %get-tuple-element.36), channel_id=1, source_target_pairs={{0,1},{1,2},{2,3},{3,4},{4,5},{5,6},{6,7},{7,8},{8,9},{9,10},{10,1... | collective-permute-start | bytes 1572872 | tf_op jit(solution)/shard_map/ppermute | solution.py:19
  293.9 18.7 %collective-permute-start.9 = (f32[1,512,256]{2,1,0:T(8,128)S(1)}, f32[1,512,256]{2,1,0:T(8,128)S(1)}, u32[]{:S(2)}, u32[]{:S(2)}) collective-permute-start(f32[1,512,256]{2,1,0:T(8,128)S(1)} %get-tuple-element.37), channel_id=1, source_target_pairs={{16,0},{32,16},{48,32},{64,48},{80,64},{96,80},{112,96},{17,1},{33... | collective-permute-start | bytes 1572872 | tf_op jit(solution)/shard_map/ppermute | solution.py:22
  428.1 12.9 %collective-permute-start.12 = (f32[1,512,256]{2,1,0:T(8,128)}, f32[1,512,256]{2,1,0:T(8,128)}, u32[]{:S(2)}, u32[]{:S(2)}) collective-permute-start(f32[1,512,256]{2,1,0:T(8,128)} %get-tuple-element.30), channel_id=1, source_target_pairs={{0,16},{16,32},{32,48},{48,64},{64,80},{80,96},{96,112},{1,17},{17... | collective-permute-start | bytes 1572872 | tf_op jit(solution)/shard_map/ppermute | solution.py:19
  431.5 10.8 %collective-permute-start.15 = (f32[1,512,256]{2,1,0:T(8,128)}, f32[1,512,256]{2,1,0:T(8,128)}, u32[]{:S(2)}, u32[]{:S(2)}) collective-permute-start(f32[1,512,256]{2,1,0:T(8,128)} %get-tuple-element.31), channel_id=1, source_target_pairs={{1,0},{2,1},{3,2},{4,3},{5,4},{6,5},{7,6},{8,7},{9,8},{10,9},{11,1... | collective-permute-start | bytes 1572872 | tf_op jit(solution)/shard_map/ppermute | solution.py:22
  435.0 8.5 %collective-permute-start.14 = (f32[1,512,256]{2,1,0:T(8,128)}, f32[1,512,256]{2,1,0:T(8,128)}, u32[]{:S(2)}, u32[]{:S(2)}) collective-permute-start(f32[1,512,256]{2,1,0:T(8,128)} %get-tuple-element.32), channel_id=1, source_target_pairs={{0,1},{1,2},{2,3},{3,4},{4,5},{5,6},{6,7},{7,8},{8,9},{9,10},{10,1... | collective-permute-start | bytes 1572872 | tf_op jit(solution)/shard_map/ppermute | solution.py:19
  437.1 18.0 %collective-permute-start.13 = (f32[1,512,256]{2,1,0:T(8,128)S(1)}, f32[1,512,256]{2,1,0:T(8,128)}, u32[]{:S(2)}, u32[]{:S(2)}) collective-permute-start(f32[1,512,256]{2,1,0:T(8,128)S(1)} %get-tuple-element.33), channel_id=1, source_target_pairs={{16,0},{32,16},{48,32},{64,48},{80,64},{96,80},{112,96},{17,1},{33... | collective-permute-start | bytes 1572872 | tf_op jit(solution)/shard_map/ppermute | solution.py:22
  456.8 2.3 copy-start.2
  476.4 6.7 %copy-start.6 = (f32[2048,256]{0,1:T(8,128)}, f32[2048,256]{0,1:T(8,128)S(1)}, u32[]{:S(2)}) copy-start(f32[2048,256]{0,1:T(8,128)S(1)} %get-tuple-element.27) | copy-start | bytes 6291460
